TPU v7x, 512 devices: a whole 4x8x8 slice. The times are simulated.
512 devices in a mesh: pair: 16 (over x, y_hi, core), virt: 32 (over z, y_lo).
Axes of the slice: x: 4, y: 8 (y_hi: 2, y_lo: 4; y = y_hi * 4 + y_lo), z: 8, core: 2. Of those that a mesh axis runs over, the one named last changes fastest.
Arguments:
- amplitudes: bfloat16 [16384, 1024], P(('pair', 'virt')), may hold values from -6 to 6
- integrals: bfloat16 [1024, 65536], P('pair', 'virt'), may hold values from -0.1875 to 0.1875
- amp_mask: int32 [256, 16], P('pair'), may hold values from 0 to 1, as said below
- integral_mask: int32 [16, 1024], P('pair', 'virt'), may hold values 0 or 1
Outputs:
- ladder: bfloat16 [16384, 65536], P('pair', 'virt')
Inputs may be any that keep to these rules, and one draw needn't show every extreme that they name: `amp_mask`: 0 or 1. For every block of 16 consecutive ij tiles, the cd tiles that hold nonzeros lie within one cyclic window of cd tiles common to the block, whose length may differ from block to block.
All inputs are finite; a program needn't handle non-finite values. No bound on the sum of `integral_mask` on one device may be relied on, other than what follows from the above.
Results may differ from a plain program's by a relative error of at most 0.001.
Values may be sent and summed in bfloat16 or wider, within the bound.
No kernel may reach another device: no remote copies, remote signals or barrier semaphores. Data moves between devices by JAX's collectives and lax.ppermute only.
A program may use at most 64 MiB of HBM per device.

v0:
```python
import jax
import jax.numpy as jnp
from jax import lax
from jax.sharding import PartitionSpec as P

TILE = 64


def widened_mask(values, mask):
    tile_rows, tile_columns = mask.shape
    shaped = values.reshape(tile_rows, TILE, tile_columns, TILE)
    return (shaped * mask.astype(values.dtype)[:, None, :, None]).reshape(values.shape)


def on_device(amplitudes, integrals, amp_mask, integral_mask):
    full_amp = lax.all_gather(amplitudes, "virt", axis=0, tiled=True)
    masked_amp = widened_mask(full_amp, amp_mask)
    own_panel = widened_mask(integrals, integral_mask)
    whole_panel = lax.all_gather(own_panel, "pair", axis=0, tiled=True)
    result = jnp.dot(masked_amp, whole_panel, preferred_element_type=jnp.float32)
    return result.astype(jnp.bfloat16)


def solution(mesh):
    in_specs = (P(("pair", "virt"), None), P("pair", "virt"), P("pair", None), P("pair", "virt"))
    out_specs = P("pair", "virt")
    return jax.shard_map(
        on_device, mesh=mesh, in_specs=in_specs, out_specs=out_specs, check_vma=False
    )
```

profile of v0, /device:TPU:1, one launch (start us, length us, event | category | flops | bytes accessed | tf_op | source)
XLA Modules:
  0.0 274.7 jit_solution(16566469928729654126)
XLA Ops:
  6.5 0.0 all-gather.3.cloned.1.call-start
  6.5 0.7 all-gather.3.cloned.1.call-update
  7.3 0.0 all-gather.5.cloned.1.call-start
  7.3 0.7 convert_bitcast_fusion
  8.0 0.1 mul.32
  8.0 0.1 mul.33
  8.1 1.7 broadcast_multiply_fusion
  9.8 0.0 all-gather.5.cloned.1.call-update
  9.8 0.7 convert_element_type.9
  10.5 2.6 mul.28
  13.1 5.5 %mul.29 = bf16[1024,1024]{1,0:T(8,128)(2,1)S(1)} reshape(bf16[16,64,16,64]{3,2,1,0:T(8,128)(2,1)} %mul.28) | data formatting | bytes 4194304 | tf_op jit(solution)/shard_map/mul | solution.py:12
  18.6 134.1 %all-gather.3.cloned.1.call-done = bf16[1024,1024]{1,0:T(8,128)(2,1)} async-done(((bf16[32,1024]{1,0:T(8,128)(2,1)}), bf16[1024,1024]{1,0:T(8,128)(2,1)}) %all-gather.3.cloned.1.call-update) | async-done | bytes 2097168 | tf_op jit(solution)/shard_map/all_gather | solution.py:16
  152.8 105.7 %all-gather.5.cloned.1.call-done = bf16[1024,2048]{1,0:T(8,128)(2,1)} async-done(((bf16[64,2048]{1,0:T(8,128)(2,1)}), bf16[1024,2048]{1,0:T(8,128)(2,1)}) %all-gather.5.cloned.1.call-update) | async-done | bytes 4194320 | tf_op jit(solution)/shard_map/all_gather | solution.py:19
  258.5 9.3 %convolution_convert_fusion = bf16[1024,2048]{1,0:T(8,128)(2,1)} fusion(bf16[1024,2048]{1,0:T(8,128)(2,1)} %all-gather.5.cloned.1.call-done, bf16[1024,1024]{1,0:T(8,128)(2,1)} %all-gather.3.cloned.1.call-done, bf16[1024,1024]{1,0:T(8,128)(2,1)S(1)} %mul.29), kind=kOutput, calls=%fused_computation | convolution fusion | flops 4298113024 | bytes 12582912 | tf_op jit(solution)/shard_map/dot_general | solution.py:20
Async XLA Ops:
  6.5 146.2 %all-gather.3.cloned.1.call-start = ((), (), s32[]{:S(2)}) async-start(), calls=%async_computation | async-start | bytes 2162688 | tf_op jit(solution)/shard_map/all_gather | solution.py:16
  7.3 251.2 %all-gather.5.cloned.1.call-start = ((), (), s32[]{:S(2)}) async-start(), calls=%async_computation.1 | async-start | bytes 4456448 | tf_op jit(solution)/shard_map/all_gather | solution.py:19
Sparse Core Ops, SparseCore 0:
  9.4 143.3 all-gather.2
  156.0 102.4 all-gather.4
where the time goes:
time: 275 us
  waiting for transfers between devices  241 us (88%)
  between operations  13.4 us (5%)
  matrix products  9.34 us (3%)
  local copies, waits for them, and re-layouts  8.26 us (3%)
  other arithmetic  3.02 us (1%)
    all_gather x1, waiting for transfers between devices, on_device(): full_amp = lax.all_gather(amplitudes, 'virt', axis=0, tiled=True)  134 us
    all_gather x1, waiting for transfers between devices, on_device(): whole_panel = lax.all_gather(own_panel, 'pair', axis=0, tiled=True)  106 us
    dot_general x1, matrix products, on_device(): jnp.dot(masked_amp, whole_panel, preferred_element_type=jnp.float32)  9.34 us
    mul x4, local copies, waits for them, and re-layouts, widened_mask(): shaped * mask.astype(values.dtype)[:, None, :, None]  8.26 us
  transfers between devices with their start and end apart: 2, of which 2 were waited for; matrix products, arithmetic and copies ran while one was open for 4% of the time, Pallas kernels for 0%

commit v1 on v0

--- a/solution.py
+++ b/solution.py
@@ -4,6 +4,10 @@
 from jax.sharding import PartitionSpec as P
 
 TILE = 64
+begin_the_series_all = lambda message: jnp.concatenate(
+    lax.all_to_all(jnp.stack([message for _ in range(lax.axis_size("pair"))], 0), "pair", 0, 0),
+    axis=0,
+)
 
 
 def widened_mask(values, mask):
@@ -16,7 +20,7 @@
     full_amp = lax.all_gather(amplitudes, "virt", axis=0, tiled=True)
     masked_amp = widened_mask(full_amp, amp_mask)
     own_panel = widened_mask(integrals, integral_mask)
-    whole_panel = lax.all_gather(own_panel, "pair", axis=0, tiled=True)
+    whole_panel = begin_the_series_all(own_panel)
     result = jnp.dot(masked_amp, whole_panel, preferred_element_type=jnp.float32)
     return result.astype(jnp.bfloat16)
 

time: 275 us -> 221 us (0.80)
  the two profiles are of different devices: /device:TPU:1 before, /device:TPU:2 now
where the time goes in v1:
time: 221 us; the launch traced here: 220 us
  waiting for transfers between devices  175 us (79%)
  between operations  13.4 us (6%)
  local copies, waits for them, and re-layouts  10.8 us (5%)
  starting transfers between devices  10.3 us (5%)
  matrix products  9.34 us (4%)
    all_gather x1, waiting for transfers between devices, on_device(): full_amp = lax.all_gather(amplitudes, 'virt', axis=0, tiled=True)  174 us
    all_to_all x1, starting transfers between devices, lax.all_to_all(jnp.stack([message for _ in range(lax.axis_size('pair'))],...  10.3 us
    dot_general x1, matrix products, on_device(): jnp.dot(masked_amp, whole_panel, preferred_element_type=jnp.float32)  9.34 us
    mul x4, local copies, waits for them, and re-layouts, widened_mask(): shaped * mask.astype(values.dtype)[:, None, :, None]  8.22 us
  transfers between devices with their start and end apart: 2, of which 1 were waited for; matrix products, arithmetic and copies ran while one was open for 4% of the time, Pallas kernels for 0%

profile of v1, /device:TPU:2, one launch (start us, length us, event | category | flops | bytes accessed | tf_op | source)
XLA Modules:
  0.0 220.2 jit_solution(8721759565722545066)
XLA Ops:
  6.5 0.7 convert_bitcast_fusion
  7.2 0.1 mul.33
  7.3 0.1 mul.34
  7.4 1.0 broadcast_multiply_fusion
  8.3 2.5 %stack.3 = bf16[16,64,2048]{2,1,0:T(8,128)(2,1)} broadcast(bf16[64,2048]{1,0:T(8,128)(2,1)S(1)} %broadcast_multiply_fusion), dimensions={1,2} | broadcast | bytes 4456448 | tf_op jit(solution)/shard_map/stack | solution.py:8
  10.9 0.0 copy-start
  10.9 10.3 %all-to-all-start = ((bf16[16,64,2048]{2,1,0:T(8,128)(2,1)}), bf16[16,64,2048]{2,1,0:T(8,128)(2,1)}, u32[]{:S(2)}, u32[]{:S(2)}) async-start(bf16[16,64,2048]{2,1,0:T(8,128)(2,1)} %stack.3), calls=%async_computation | async-start | bytes 8388608 | tf_op jit(solution)/shard_map/all_to_all | solution.py:8
  21.2 0.0 all-gather.2.cloned.1.call-start
  21.2 0.7 all-gather.2.cloned.1.call-update
  21.9 0.0 copy-done
  21.9 2.6 %mul.29 = bf16[16,64,16,64]{3,2,1,0:T(8,128)(2,1)} broadcast(bf16[16,16]{1,0:T(8,128)(2,1)S(1)} %convert_element_type.9), dimensions={0,2} | broadcast | bytes 2097664 | tf_op jit(solution)/shard_map/mul | solution.py:16
  24.5 5.5 %mul.30 = bf16[1024,1024]{1,0:T(8,128)(2,1)S(1)} reshape(bf16[16,64,16,64]{3,2,1,0:T(8,128)(2,1)} %mul.29) | data formatting | bytes 4194304 | tf_op jit(solution)/shard_map/mul | solution.py:16
  30.0 174.0 %all-gather.2.cloned.1.call-done = bf16[1024,1024]{1,0:T(8,128)(2,1)} async-done(((bf16[32,1024]{1,0:T(8,128)(2,1)}), bf16[1024,1024]{1,0:T(8,128)(2,1)}) %all-gather.2.cloned.1.call-update) | async-done | bytes 2097168 | tf_op jit(solution)/shard_map/all_gather | solution.py:20
  204.0 0.0 all-to-all-done
  204.0 9.3 %convolution_convert_fusion = bf16[1024,2048]{1,0:T(8,128)(2,1)} fusion(bf16[1024,2048]{1,0:T(8,128)(2,1)} %bitcast.1, bf16[1024,1024]{1,0:T(8,128)(2,1)} %all-gather.2.cloned.1.call-done, bf16[1024,1024]{1,0:T(8,128)(2,1)S(1)} %mul.30), kind=kOutput, calls=%fused_computation | convolution fusion | flops 4298113024 | bytes 12582912 | tf_op jit(solution)/shard_map/dot_general | solution.py:24
  (1 shorter events, 0.0 us)
Async XLA Ops:
  10.9 11.0 %copy-start = (s32[16,16]{1,0:T(8,128)S(1)}, s32[16,16]{1,0:T(8,128)}, u32[]{:S(2)}) copy-start(s32[16,16]{1,0:T(8,128)} %param.6) | copy-start | bytes 3076
  10.9 193.2 %all-to-all-start = ((bf16[16,64,2048]{2,1,0:T(8,128)(2,1)}), bf16[16,64,2048]{2,1,0:T(8,128)(2,1)}, u32[]{:S(2)}, u32[]{:S(2)}) async-start(bf16[16,64,2048]{2,1,0:T(8,128)(2,1)} %stack.3), calls=%async_computation | async-start | bytes 8388608 | tf_op jit(solution)/shard_map/all_to_all | solution.py:8
  21.2 182.9 %all-gather.2.cloned.1.call-start = ((), (), s32[]{:S(2)}) async-start(), calls=%async_computation.1 | async-start | bytes 2162688 | tf_op jit(solution)/shard_map/all_gather | solution.py:20
Sparse Core Ops, SparseCore 0:
  24.1 179.9 all-gather.1
